TPU v7x, 32 devices: a whole 2x2x4 slice. The times are simulated.
32 devices in a mesh: seq: 8 (over y, x, core), head: 4 (over z).
Axes of the slice: x: 2, y: 2, z: 4, core: 2. Of those that a mesh axis runs over, the one named last changes fastest.
Arguments:
- queries: bfloat16 [3, 2048, 2048], P(None, 'seq', 'head'), may hold values from -24 to 24
- key_vectors: bfloat16 [4, 2048, 2048], P(None, 'seq', 'head'), may hold values from -24 to 24
- values: bfloat16 [4, 2048, 2048], P(None, 'seq', 'head'), may hold values from -6 to 6
- learn_rates: float32 [3, 2048, 4], P(None, 'seq', 'head'), may hold values from 0.001 to 0.01
- norm_gain: float32 [2048], P('head'), may hold values from 0.1 to 1.9
- out_weight: bfloat16 [2048, 2048], P('head'), may hold values from -0.125 to 0.125
- incoming: float32 [8, 4, 3, 512, 512], P('seq', 'head'), may hold values from -0.25 to 0.25
Outputs:
- mixed_out: bfloat16 [3, 2048, 2048], P(None, 'seq', 'head')
- outgoing: float32 [8, 4, 3, 512, 512], P('seq', 'head')
All inputs are finite; a program needn't handle non-finite values.
Results may differ from a plain program's by a relative error of at most 0.013.
The roundings to bfloat16 on the way count: a program that leaves them out, or rounds other values in their place, can miss the bound.
Values may be sent and summed in bfloat16 or wider, within the bound.
A program may use at most 64 MiB of HBM per device.

v0:
```python
import functools

import jax
import jax.numpy as jnp
from jax import lax
from jax.experimental import pallas as pl
from jax.experimental.pallas import tpu as pltpu
from jax.sharding import PartitionSpec as P


F32, BF16 = jnp.float32, jnp.bfloat16
MESH = pl.DeviceIdType.MESH
WEIGHTS = (0, 1, 2)
LATE_PIECES = 2


def dot(a, b, over=(1, 0)):
    return lax.dot_general(a, b, (((over[0],), (over[1],)), ((), ())), preferred_element_type=F32)


def normed_apply(rounded, query_rows, gain_row):
    first_proj = dot(query_rows, rounded[0]())
    third_proj = dot(query_rows, rounded[1]())
    hidden = (first_proj * jax.nn.sigmoid(first_proj) * third_proj).astype(BF16)
    fast_out = dot(hidden, rounded[2]())
    mean_sq = jnp.mean(fast_out * fast_out, axis=1, keepdims=True)
    return fast_out * lax.rsqrt(mean_sq + 1e-06) * gain_row


def fast_update(olds, rounded, key_rows, scaled_values, put_new):
    first_proj = dot(key_rows, rounded[0]())
    third_proj = dot(key_rows, rounded[1]())
    gate_sig = jax.nn.sigmoid(first_proj)
    gated = first_proj * gate_sig

    def put(i, grad):
        old = olds[i]()
        stepped = old + grad
        before_sq = jnp.mean(old * old, axis=0, keepdims=True)
        after_sq = jnp.mean(stepped * stepped, axis=0, keepdims=True)
        put_new(i, stepped * jnp.sqrt((before_sq + 1e-06) / (after_sq + 1e-06)))

    back_grad = dot(scaled_values, rounded[2](), (1, 1))
    slope = gate_sig * (1.0 + first_proj * (1.0 - gate_sig))
    put(0, dot(key_rows, (back_grad * third_proj * slope).astype(BF16), (0, 0)))
    put(1, dot(key_rows, (back_grad * gated).astype(BF16), (0, 0)))
    hidden = (gated * third_proj).astype(BF16)
    put(2, dot(hidden, scaled_values, (0, 0)))


def softmax_parts(scores, own):
    expo = jnp.exp(scores - jnp.max(scores, axis=1, keepdims=True))
    probs = expo / jnp.sum(expo, axis=1, keepdims=True)
    zero = jnp.zeros_like(probs)
    return jnp.where(own, probs, zero).astype(BF16), jnp.where(own, zero, probs).astype(BF16)


def attend_rows(query_rows, prior, own, low, high):
    size = query_rows.shape[1]
    length = own.length
    scale = size ** (-0.5)
    span = high - low
    pieces = []
    if low:
        pieces.append(dot(query_rows, own.keys(0, low), (1, 1)))
    row = lax.broadcasted_iota(jnp.int32, (span, span), 0)
    col = lax.broadcasted_iota(jnp.int32, (span, span), 1)
    pieces.append(
        jnp.where(
            col <= row,
            dot(query_rows, own.keys(low, high), (1, 1)),
            dot(query_rows, prior.keys(low, high), (1, 1)),
        )
    )
    if high < length:
        pieces.append(dot(query_rows, prior.keys(high, length), (1, 1)))
    scores = (jnp.concatenate(pieces, axis=1) if len(pieces) > 1 else pieces[0]) * scale
    row = lax.broadcasted_iota(jnp.int32, (span, length), 0) + low
    is_own = lax.broadcasted_iota(jnp.int32, (span, length), 1) <= row
    own_probs, prior_probs = softmax_parts(scores, is_own)
    return dot(own_probs[:, :high], own.values(0, high)) + dot(
        prior_probs[:, low:], prior.values(low, length)
    )


class Rows:
    def __init__(self, keys_ref, values_ref):
        self.k, self.v, self.length = keys_ref, values_ref, keys_ref.shape[0]

    def keys(self, a, b):
        return self.k[a:b]

    def values(self, a, b):
        return self.v[a:b]


def layer_kernel(
    q_hbm, k_hbm, v_hbm, rate_hbm, gain_hbm, ow_hbm, w_hbm,
    out_ref, new_ref,
    q, k, v, rate, gain, ow, w,
    near, w_send, w_recv, z_send, z_recv, z_keep, z_fwd, z_last, z_own,
    in_sem, near_s, near_r, w_s, w_r, z1_s, z1_r, z2_s, z2_r,
):
    ticks, rows, size = q.shape
    last = ticks - 1
    n_seq, n_head = lax.axis_size("seq"), lax.axis_size("head")
    s, h = lax.axis_index("seq"), lax.axis_index("head")
    nxt, prv = lax.rem(s + 1, n_seq), lax.rem(s + n_seq - 1, n_seq)
    odd = lax.rem(s, 2)
    side = h + 1 - 2 * lax.rem(h, 2)
    mirror = n_head - 1 - h
    across = lax.rem(h + n_head // 2, n_head)
    first = side + odd * (mirror - side)
    second = mirror + odd * (side - mirror)

    loads = []

    def load(src, dst):
        copy = pltpu.make_async_copy(src, dst, in_sem.at[len(loads)])
        copy.start()
        loads.append(copy)
        return copy

    get_k = [None] * ticks
    get_v = [None] * ticks
    get_q = [None] * ticks
    get_k[0] = load(k_hbm.at[1], k.at[0])
    get_w = [load(w_hbm.at[0, 0, i], w.at[i]) for i in WEIGHTS]
    get_v[0] = load(v_hbm.at[1], v.at[0])
    get_rate = load(rate_hbm, rate)

    barrier = pltpu.get_barrier_semaphore()
    for who in ({"seq": nxt}, {"seq": prv}, {"head": side}, {"head": mirror}):
        pl.semaphore_signal(barrier, inc=1, device_id=who, device_id_type=MESH)

    get_q[0] = load(q_hbm.at[0], q.at[0])
    get_gain = load(gain_hbm, gain)
    get_ow = load(ow_hbm, ow)
    for t in range(1, ticks):
        get_k[t] = load(k_hbm.at[t + 1], k.at[t])
        get_v[t] = load(v_hbm.at[t + 1], v.at[t])
        get_q[t] = load(q_hbm.at[t], q.at[t])
    pl.semaphore_wait(barrier, 4)

    sent = []

    def remote(src, dst, ss, rs, who):
        return pltpu.make_async_remote_copy(
            src_ref=src, dst_ref=dst, send_sem=ss, recv_sem=rs, device_id=who, device_id_type=MESH
        )

    def push(copy):
        copy.start()
        sent.append(copy)

    step = rows // LATE_PIECES

    def near_copies(t):
        cuts = [(0, rows)] if t < last else [(i * step, (i + 1) * step) for i in reversed(range(LATE_PIECES))]
        found = []
        for j, (a, b) in enumerate(cuts):
            for i, hbm in enumerate((k_hbm, v_hbm)):
                at = (t, j, i)
                found.append(
                    remote(
                        hbm.at[t, pl.ds(a, b - a)], near.at[t, i, pl.ds(a, b - a)],
                        near_s.at[at], near_r.at[at], {"seq": nxt},
                    )
                )
        return found

    def send_near(t):
        for copy in near_copies(t):
            push(copy)

    def w_copy(t, i):
        return remote(w_send.at[t, i], w_recv.at[t, i], w_s.at[t, i], w_r.at[t, i], {"seq": nxt})

    def sv_of(t):
        column = jnp.broadcast_to(rate[t : t + 1], (8, rows)).T[:, :1]
        return (column * v[t].astype(F32)).astype(BF16)

    def z_first(t, a, b, j, i):
        return remote(
            z_send.at[t, i, pl.ds(a, b - a)], z_recv.at[t, i, pl.ds(a, b - a)],
            z1_s.at[t, j, i], z1_r.at[t, j, i], {"head": first},
        )

    def z_second(t, a, b, j):
        return remote(
            z_fwd.at[t, pl.ds(a, b - a)], z_last.at[t, pl.ds(a, b - a)],
            z2_s.at[t, j], z2_r.at[t, j], {"head": second},
        )

    def project(combined, t, a, b, j):
        def piece(target):
            columns = pl.ds(pl.multiple_of(target * size, 128), size)
            return dot(combined, ow[:, columns]).astype(BF16)

        for i, target in enumerate((across, first)):
            z_send[t, i, a:b] = piece(target)
            push(z_first(t, a, b, j, i))
        z_keep[t, 0, a:b] = piece(second)
        z_keep[t, 1, a:b] = piece(h)

    def pass_on(t, a, b, j):
        z_first(t, a, b, j, 0).wait_recv()
        z_fwd[t, a:b] = (z_keep[t, 0, a:b].astype(F32) + z_recv[t, 0, a:b].astype(F32)).astype(BF16)
        push(z_second(t, a, b, j))
        z_first(t, a, b, j, 1).wait_recv()
        z_own[t, a:b] = z_keep[t, 1, a:b].astype(F32) + z_recv[t, 1, a:b].astype(F32)

    def finish(t, a, b, j):
        z_second(t, a, b, j).wait_recv()
        out_ref[t, a:b] = (z_own[t, a:b] + z_last[t, a:b].astype(F32)).astype(BF16)

    def waiting(copy, read):
        done = []

        def get():
            if not done:
                copy.wait()
                done.append(True)
            return read()

        return get

    def arrived(t, i):
        done = []

        def get():
            if not done:
                w_copy(t, i).wait_recv()
                done.append(True)
            return w_recv[t, i]

        return get

    own = [Rows(k.at[t], v.at[t]) for t in range(ticks)]
    prior = [Rows(near.at[t, 0], near.at[t, 1]) for t in range(ticks)]
    state = [waiting(get_w[i], lambda i=i: w[i]) for i in WEIGHTS]
    rounded = [lambda i=i: state[i]().astype(BF16) for i in WEIGHTS]
    send_near(0)

    for t in range(ticks):
        get_k[t].wait()
        get_v[t].wait()
        if t == 0:
            get_rate.wait()

        def update():
            def store(i, x):
                if t < last:
                    w_send[t, i] = x.astype(BF16)
                    push(w_copy(t, i))
                else:
                    new_ref[0, 0, i] = x

            fast_update(state, rounded, k[t], sv_of(t), store)
            if t < last:
                send_near(t + 1)

        def apply():
            get_q[t].wait()
            if t == 0:
                get_gain.wait()
            return normed_apply(rounded, q[t], gain[...])

        if t < last:
            update()
            normed = apply()
        else:
            normed = apply()
            update()
        if t == 0:
            get_ow.wait()
        if t < last:
            for copy in near_copies(t):
                copy.wait_recv()
            att = attend_rows(q[t], prior[t], own[t], 0, rows)
            project((att + normed).astype(BF16), t, 0, rows, 0)
            if t:
                finish(t - 1, 0, rows, 0)
            pass_on(t, 0, rows, 0)
            rounded = [arrived(t, i) for i in WEIGHTS]
            state = [lambda f=f: f().astype(F32) for f in rounded]
        else:
            finish(t - 1, 0, rows, 0)
            cuts = [(i * step, (i + 1) * step) for i in reversed(range(LATE_PIECES))]
            copies = near_copies(t)
            for j, (a, b) in enumerate(cuts):
                for copy in copies[2 * j : 2 * j + 2]:
                    copy.wait_recv()
                att = attend_rows(q[t, a:b], prior[t], own[t], a, b)
                project((att + normed[a:b]).astype(BF16), t, a, b, j)
            for j, (a, b) in enumerate(cuts):
                pass_on(t, a, b, j)
            for j, (a, b) in enumerate(cuts):
                finish(t, a, b, j)
    for copy in sent:
        copy.wait_send()


def on_device(queries, key_vectors, values, learn_rates, norm_gain, out_weight, incoming):
    ticks, rows, size = queries.shape
    any_space = pl.BlockSpec(memory_space=pl.ANY)
    vmem = pl.BlockSpec(memory_space=pltpu.VMEM)
    dma = pltpu.SemaphoreType.DMA
    block = (ticks, rows, size)
    matrices = (len(WEIGHTS), size, size)
    scratch = [
        pltpu.VMEM(block, BF16),
        pltpu.VMEM(block, BF16),
        pltpu.VMEM(block, BF16),
        pltpu.VMEM((ticks, rows), F32),
        pltpu.VMEM((1, size), F32),
        pltpu.VMEM(out_weight.shape, BF16),
        pltpu.VMEM(matrices, F32),
        pltpu.VMEM((ticks, 2, rows, size), BF16),
        pltpu.VMEM((ticks - 1, *matrices), BF16),
        pltpu.VMEM((ticks - 1, *matrices), BF16),
        pltpu.VMEM((ticks, 2, rows, size), BF16),
        pltpu.VMEM((ticks, 2, rows, size), BF16),
        pltpu.VMEM((ticks, 2, rows, size), BF16),
        pltpu.VMEM(block, BF16),
        pltpu.VMEM(block, BF16),
        pltpu.VMEM(block, F32),
        dma((6 + 3 * ticks,)),
        dma((ticks, LATE_PIECES, 2)),
        dma((ticks, LATE_PIECES, 2)),
        dma((ticks - 1, len(WEIGHTS))),
        dma((ticks - 1, len(WEIGHTS))),
        dma((ticks, LATE_PIECES, 2)),
        dma((ticks, LATE_PIECES, 2)),
        dma((ticks, LATE_PIECES)),
        dma((ticks, LATE_PIECES)),
    ]
    out, outgoing = pl.pallas_call(
        layer_kernel,
        out_shape=[
            jax.ShapeDtypeStruct(queries.shape, BF16),
            jax.ShapeDtypeStruct(incoming.shape, F32),
        ],
        in_specs=[any_space] * 7,
        out_specs=[vmem, vmem],
        scratch_shapes=scratch,
        compiler_params=pltpu.CompilerParams(
            collective_id=0, has_side_effects=True, vmem_limit_bytes=60 << 20
        ),
        name="layer_kernel",
    )(
        queries, key_vectors, values, learn_rates.reshape(ticks, rows), norm_gain.reshape(1, size),
        out_weight, incoming,
    )
    return out, outgoing


def solution(mesh):
    placed = (
        P(None, "seq", "head"),
        P(None, "seq", "head"),
        P(None, "seq", "head"),
        P(None, "seq", "head"),
        P("head"),
        P("head", None),
        P("seq", "head", None, None, None),
    )
    return jax.shard_map(
        on_device,
        mesh=mesh,
        in_specs=placed,
        out_specs=(P(None, "seq", "head"), P("seq", "head", None, None, None)),
        check_vma=False,
    )
```

profile of v0, /device:TPU:0, one launch (start us, length us, event | category | flops | bytes accessed | tf_op | source)
XLA Modules:
  0.0 84.4 jit_solution(15735115972640865362)
XLA Ops:
  0.6 1.3 %copy.11 = f32[3,256,1]{1,0,2:T(4,128)} copy(f32[3,256,1]{1,2,0:T(1,128)} %param.10) | data formatting | bytes 6144
  1.9 76.6 %layer_kernel.1 = (bf16[3,256,512]{2,1,0:T(8,128)(2,1)}, f32[1,1,3,512,512]{4,3,2,1,0:T(8,128)}) custom-call(bf16[3,256,512]{2,1,0:T(8,128)(2,1)} %q_hbm.1, bf16[4,256,512]{2,1,0:T(8,128)(2,1)} %k_hbm.1, bf16[4,256,512]{2,1,0:T(8,128)(2,1)} %v_hbm.1, f32[3,256]{1,0:T(4,128)} %bitcast.4, f32[1,512]{1,0:T(1,128)} %bitcast.5, bf16[512,2048]{1,0:T(8,128)(2,1)} %ow_hbm.1, ...), custom_call_target="tpu_custom_call" | custom-call | tf_op jit(solution)/shard_map/layer_kernel/pallas_call | solution.py:338
  78.5 2.1 %copy.14 = bf16[3,256,512]{2,1,0:T(8,128)(2,1)} copy(bf16[3,256,512]{2,1,0:T(8,128)(2,1)} %get-tuple-element.4) | data formatting | bytes 1572864
  80.5 3.9 %copy.15 = f32[1,1,3,512,512]{4,3,2,1,0:T(8,128)} copy(f32[1,1,3,512,512]{4,3,2,1,0:T(8,128)} %get-tuple-element.5) | data formatting | bytes 6291456
where the time goes:
time: 84.6 us; the launch traced here: 84.4 us
  Pallas kernels  76.6 us (91%)
  local copies, waits for them, and re-layouts  7.2 us (9%)
    pallas_call x1, Pallas kernels, on_device(): pl.pallas_call(layer_kernel, out_shape=[jax.ShapeDtypeStruct(queries.shap...  76.6 us
    unnamed x3, local copies, waits for them, and re-layouts  7.2 us

commit v1 on v0

--- a/solution.py
+++ b/solution.py
@@ -11,7 +11,8 @@
 F32, BF16 = jnp.float32, jnp.bfloat16
 MESH = pl.DeviceIdType.MESH
 WEIGHTS = (0, 1, 2)
-LATE_PIECES = 2
+LATE_PIECES = 4
+LANES = 128
 
 
 def dot(a, b, over=(1, 0)):
@@ -55,31 +56,27 @@
     return jnp.where(own, probs, zero).astype(BF16), jnp.where(own, zero, probs).astype(BF16)
 
 
-def attend_rows(query_rows, prior, own, low, high):
-    size = query_rows.shape[1]
+def own_scores(query_rows, own):
+    return dot(query_rows, own.keys(0, own.length), (1, 1))
+
+
+def attend_rows(query_rows, scores_own, prior, own, low):
+    span, size = query_rows.shape
     length = own.length
-    scale = size ** (-0.5)
-    span = high - low
-    pieces = []
-    if low:
-        pieces.append(dot(query_rows, own.keys(0, low), (1, 1)))
-    row = lax.broadcasted_iota(jnp.int32, (span, span), 0)
-    col = lax.broadcasted_iota(jnp.int32, (span, span), 1)
-    pieces.append(
-        jnp.where(
-            col <= row,
-            dot(query_rows, own.keys(low, high), (1, 1)),
-            dot(query_rows, prior.keys(low, high), (1, 1)),
-        )
-    )
-    if high < length:
-        pieces.append(dot(query_rows, prior.keys(high, length), (1, 1)))
-    scores = (jnp.concatenate(pieces, axis=1) if len(pieces) > 1 else pieces[0]) * scale
+    reach = min(length, -(-(low + span) // LANES) * LANES)
+
+    def joined(part_own, part_prior):
+        if not low:
+            return part_prior(0, length)
+        return jnp.concatenate([part_own(0, low), part_prior(low, length)], axis=0)
+
     row = lax.broadcasted_iota(jnp.int32, (span, length), 0) + low
     is_own = lax.broadcasted_iota(jnp.int32, (span, length), 1) <= row
+    other = dot(query_rows, joined(own.keys, prior.keys), (1, 1))
+    scores = jnp.where(is_own, scores_own, other) * size ** (-0.5)
     own_probs, prior_probs = softmax_parts(scores, is_own)
-    return dot(own_probs[:, :high], own.values(0, high)) + dot(
-        prior_probs[:, low:], prior.values(low, length)
+    return dot(own_probs[:, :reach], own.values(0, reach)) + dot(
+        prior_probs, joined(own.values, prior.values)
     )
 
 
@@ -110,8 +107,7 @@
     side = h + 1 - 2 * lax.rem(h, 2)
     mirror = n_head - 1 - h
     across = lax.rem(h + n_head // 2, n_head)
-    first = side + odd * (mirror - side)
-    second = mirror + odd * (side - mirror)
+    first, second = side, mirror
 
     loads = []
 
@@ -177,7 +173,7 @@
         return remote(w_send.at[t, i], w_recv.at[t, i], w_s.at[t, i], w_r.at[t, i], {"seq": nxt})
 
     def sv_of(t):
-        column = jnp.broadcast_to(rate[t : t + 1], (8, rows)).T[:, :1]
+        column = jnp.broadcast_to(rate[t], (8, rows)).T[:, :1]
         return (column * v[t].astype(F32)).astype(BF16)
 
     def z_first(t, a, b, j, i):
@@ -206,7 +202,7 @@
     def pass_on(t, a, b, j):
         z_first(t, a, b, j, 0).wait_recv()
         z_fwd[t, a:b] = (z_keep[t, 0, a:b].astype(F32) + z_recv[t, 0, a:b].astype(F32)).astype(BF16)
-        push(z_second(t, a, b, j))
+        z_second(t, a, b, j).start()
         z_first(t, a, b, j, 1).wait_recv()
         z_own[t, a:b] = z_keep[t, 1, a:b].astype(F32) + z_recv[t, 1, a:b].astype(F32)
 
@@ -274,36 +270,47 @@
             update()
         if t == 0:
             get_ow.wait()
+        scores_own = own_scores(q[t], own[t])
         if t < last:
             for copy in near_copies(t):
                 copy.wait_recv()
-            att = attend_rows(q[t], prior[t], own[t], 0, rows)
+            att = attend_rows(q[t], scores_own, prior[t], own[t], 0)
             project((att + normed).astype(BF16), t, 0, rows, 0)
-            if t:
+            if t == 0:
+                pl.when(odd == 0)(lambda: pass_on(0, 0, rows, 0))
+            else:
+                if t == 1:
+                    pl.when(odd == 1)(lambda: pass_on(0, 0, rows, 0))
                 finish(t - 1, 0, rows, 0)
-            pass_on(t, 0, rows, 0)
+                pass_on(t, 0, rows, 0)
             rounded = [arrived(t, i) for i in WEIGHTS]
             state = [lambda f=f: f().astype(F32) for f in rounded]
         else:
-            finish(t - 1, 0, rows, 0)
             cuts = [(i * step, (i + 1) * step) for i in reversed(range(LATE_PIECES))]
             copies = near_copies(t)
             for j, (a, b) in enumerate(cuts):
                 for copy in copies[2 * j : 2 * j + 2]:
                     copy.wait_recv()
-                att = attend_rows(q[t, a:b], prior[t], own[t], a, b)
+                att = attend_rows(q[t, a:b], scores_own[a:b], prior[t], own[t], a)
                 project((att + normed[a:b]).astype(BF16), t, a, b, j)
-            for j, (a, b) in enumerate(cuts):
-                pass_on(t, a, b, j)
+                if j == 0:
+                    finish(t - 1, 0, rows, 0)
+                if j > 1:
+                    pass_on(t, *cuts[j - 2], j - 2)
+            for j in range(LATE_PIECES - 2, LATE_PIECES):
+                pass_on(t, *cuts[j], j)
             for j, (a, b) in enumerate(cuts):
                 finish(t, a, b, j)
     for copy in sent:
         copy.wait_send()
+    for t in range(ticks):
+        for j, (a, b) in enumerate(cuts if t == last else [(0, rows)]):
+            z_second(t, a, b, j).wait_send()
 
 
 def on_device(queries, key_vectors, values, learn_rates, norm_gain, out_weight, incoming):
     ticks, rows, size = queries.shape
-    any_space = pl.BlockSpec(memory_space=pl.ANY)
+    hbm = pl.BlockSpec(memory_space=pltpu.HBM)
     vmem = pl.BlockSpec(memory_space=pltpu.VMEM)
     dma = pltpu.SemaphoreType.DMA
     block = (ticks, rows, size)
@@ -312,7 +319,7 @@
         pltpu.VMEM(block, BF16),
         pltpu.VMEM(block, BF16),
         pltpu.VMEM(block, BF16),
-        pltpu.VMEM((ticks, rows), F32),
+        pltpu.VMEM((ticks, 1, rows), F32),
         pltpu.VMEM((1, size), F32),
         pltpu.VMEM(out_weight.shape, BF16),
         pltpu.VMEM(matrices, F32),
@@ -335,23 +342,24 @@
         dma((ticks, LATE_PIECES)),
         dma((ticks, LATE_PIECES)),
     ]
+    args = (
+        queries, key_vectors, values, learn_rates.transpose(0, 2, 1), norm_gain.reshape(1, size),
+        out_weight, incoming,
+    )
     out, outgoing = pl.pallas_call(
         layer_kernel,
         out_shape=[
             jax.ShapeDtypeStruct(queries.shape, BF16),
             jax.ShapeDtypeStruct(incoming.shape, F32),
         ],
-        in_specs=[any_space] * 7,
+        in_specs=[hbm] * 7,
         out_specs=[vmem, vmem],
         scratch_shapes=scratch,
         compiler_params=pltpu.CompilerParams(
-            collective_id=0, has_side_effects=True, vmem_limit_bytes=60 << 20
+            collective_id=0, has_side_effects=True, vmem_limit_bytes=44 << 20
         ),
         name="layer_kernel",
-    )(
-        queries, key_vectors, values, learn_rates.reshape(ticks, rows), norm_gain.reshape(1, size),
-        out_weight, incoming,
-    )
+    )(*(pltpu.with_memory_space_constraint(x, pltpu.HBM) for x in args))
     return out, outgoing
 
 

time: 84.6 us -> 73.6 us (0.87)
  Pallas kernels: 76.6 us -> 70.3 us
  local copies, waits for them, and re-layouts: 7.2 us -> 2.55 us
    pallas_call x1, Pallas kernels: 76.6 us -> 70.3 us  [on_device(): pl.pallas_call(layer_kernel, out_shape=[jax.ShapeDtypeStruct(queries.shap...]
    unnamed x3 -> x2, local copies, waits for them, and re-layouts: 7.2 us -> 2.55 us
where the time goes in v1:
time: 73.6 us; the launch traced here: 73.5 us
  Pallas kernels  70.3 us (96%)
  local copies, waits for them, and re-layouts  2.55 us (3%)
    pallas_call x1, Pallas kernels, on_device(): pl.pallas_call(layer_kernel, out_shape=[jax.ShapeDtypeStruct(queries.shap...  70.3 us
    unnamed x2, local copies, waits for them, and re-layouts  2.55 us

profile of v1, /device:TPU:0, one launch (start us, length us, event | category | flops | bytes accessed | tf_op | source)
XLA Modules:
  0.0 73.5 jit_solution(17678685601044209049)
XLA Ops:
  0.6 70.3 %layer_kernel.1 = (bf16[3,256,512]{2,1,0:T(8,128)(2,1)S(1)}, f32[1,1,3,512,512]{4,3,2,1,0:T(8,128)S(1)}) custom-call(bf16[3,256,512]{2,1,0:T(8,128)(2,1)} %q_hbm.1, bf16[4,256,512]{2,1,0:T(8,128)(2,1)} %k_hbm.1, bf16[4,256,512]{2,1,0:T(8,128)(2,1)} %v_hbm.1, f32[3,1,256]{2,1,0:T(1,128)} %bitcast.2, f32[1,512]{1,0:T(1,128)} %bitcast.3, ...), custom_call_target="tpu_custom_call" | custom-call | tf_op jit(solution)/shard_map/layer_kernel/pallas_call | solution.py:349
  70.9 0.9 %copy.11 = bf16[3,256,512]{2,1,0:T(8,128)(2,1)} copy(bf16[3,256,512]{2,1,0:T(8,128)(2,1)S(1)} %get-tuple-element.4) | data formatting | bytes 1572864
  71.8 1.7 %copy.12 = f32[1,1,3,512,512]{4,3,2,1,0:T(8,128)} copy(f32[1,1,3,512,512]{4,3,2,1,0:T(8,128)S(1)} %get-tuple-element.5) | data formatting | bytes 6291456

commit v2 on v1

--- a/solution.py
+++ b/solution.py
@@ -95,8 +95,8 @@
     q_hbm, k_hbm, v_hbm, rate_hbm, gain_hbm, ow_hbm, w_hbm,
     out_ref, new_ref,
     q, k, v, rate, gain, ow, w,
-    near, w_send, w_recv, z_send, z_recv, z_keep, z_fwd, z_last, z_own,
-    in_sem, near_s, near_r, w_s, w_r, z1_s, z1_r, z2_s, z2_r,
+    near, w_send, w_recv, z_send, z_recv, z_keep, z_fwd, z_last, z_own, out, new,
+    in_sem, out_sem, near_s, near_r, w_s, w_r, z1_s, z1_r, z2_s, z2_r,
 ):
     ticks, rows, size = q.shape
     last = ticks - 1
@@ -150,11 +150,17 @@
         sent.append(copy)
 
     step = rows // LATE_PIECES
+    cuts = [(i * step, (i + 1) * step) for i in reversed(range(LATE_PIECES))]
+    leaving = []
+
+    def leave(src, dst):
+        copy = pltpu.make_async_copy(src, dst, out_sem.at[len(leaving)])
+        copy.start()
+        leaving.append(copy)
 
     def near_copies(t):
-        cuts = [(0, rows)] if t < last else [(i * step, (i + 1) * step) for i in reversed(range(LATE_PIECES))]
         found = []
-        for j, (a, b) in enumerate(cuts):
+        for j, (a, b) in enumerate(cuts if t == last else [(0, rows)]):
             for i, hbm in enumerate((k_hbm, v_hbm)):
                 at = (t, j, i)
                 found.append(
@@ -208,7 +214,9 @@
 
     def finish(t, a, b, j):
         z_second(t, a, b, j).wait_recv()
-        out_ref[t, a:b] = (z_own[t, a:b] + z_last[t, a:b].astype(F32)).astype(BF16)
+        out[t, a:b] = (z_own[t, a:b] + z_last[t, a:b].astype(F32)).astype(BF16)
+        piece = pl.ds(a, b - a)
+        leave(out.at[t, piece], out_ref.at[t, piece])
 
     def waiting(copy, read):
         done = []
@@ -250,7 +258,8 @@
                     w_send[t, i] = x.astype(BF16)
                     push(w_copy(t, i))
                 else:
-                    new_ref[0, 0, i] = x
+                    new[i] = x
+                    leave(new.at[i], new_ref.at[0, 0, i])
 
             fast_update(state, rounded, k[t], sv_of(t), store)
             if t < last:
@@ -264,29 +273,22 @@
 
         if t < last:
             update()
-            normed = apply()
-        else:
-            normed = apply()
-            update()
+        normed = apply()
         if t == 0:
             get_ow.wait()
         scores_own = own_scores(q[t], own[t])
         if t < last:
+            if t == 1:
+                pl.when(odd == 0)(lambda: pass_on(0, 0, rows, 0))
             for copy in near_copies(t):
                 copy.wait_recv()
             att = attend_rows(q[t], scores_own, prior[t], own[t], 0)
             project((att + normed).astype(BF16), t, 0, rows, 0)
-            if t == 0:
-                pl.when(odd == 0)(lambda: pass_on(0, 0, rows, 0))
-            else:
-                if t == 1:
-                    pl.when(odd == 1)(lambda: pass_on(0, 0, rows, 0))
-                finish(t - 1, 0, rows, 0)
-                pass_on(t, 0, rows, 0)
+            if t == 1:
+                pl.when(odd == 1)(lambda: pass_on(0, 0, rows, 0))
             rounded = [arrived(t, i) for i in WEIGHTS]
             state = [lambda f=f: f().astype(F32) for f in rounded]
         else:
-            cuts = [(i * step, (i + 1) * step) for i in reversed(range(LATE_PIECES))]
             copies = near_copies(t)
             for j, (a, b) in enumerate(cuts):
                 for copy in copies[2 * j : 2 * j + 2]:
@@ -294,13 +296,17 @@
                 att = attend_rows(q[t, a:b], scores_own[a:b], prior[t], own[t], a)
                 project((att + normed[a:b]).astype(BF16), t, a, b, j)
                 if j == 0:
-                    finish(t - 1, 0, rows, 0)
-                if j > 1:
-                    pass_on(t, *cuts[j - 2], j - 2)
-            for j in range(LATE_PIECES - 2, LATE_PIECES):
-                pass_on(t, *cuts[j], j)
+                    for early in range(1, last):
+                        pass_on(early, 0, rows, 0)
+            update()
+            for early in range(last):
+                finish(early, 0, rows, 0)
+            for j, (a, b) in enumerate(cuts):
+                pass_on(t, a, b, j)
             for j, (a, b) in enumerate(cuts):
                 finish(t, a, b, j)
+    for copy in leaving:
+        copy.wait()
     for copy in sent:
         copy.wait_send()
     for t in range(ticks):
@@ -308,10 +314,20 @@
             z_second(t, a, b, j).wait_send()
 
 
+def write_kernel(out_ref, new_ref, out_to, new_to, sem):
+    pairs = [(new_ref.at[0, 0, i], new_to.at[0, 0, i]) for i in range(new_ref.shape[2])]
+    pairs += [(out_ref.at[t], out_to.at[t]) for t in range(out_ref.shape[0])]
+    copies = [pltpu.make_async_copy(a, b, sem.at[i]) for i, (a, b) in enumerate(pairs)]
+    for copy in copies:
+        copy.start()
+    for copy in copies:
+        copy.wait()
+
+
 def on_device(queries, key_vectors, values, learn_rates, norm_gain, out_weight, incoming):
     ticks, rows, size = queries.shape
     hbm = pl.BlockSpec(memory_space=pltpu.HBM)
-    vmem = pl.BlockSpec(memory_space=pltpu.VMEM)
+    anywhere = pl.BlockSpec(memory_space=pl.ANY)
     dma = pltpu.SemaphoreType.DMA
     block = (ticks, rows, size)
     matrices = (len(WEIGHTS), size, size)
@@ -332,7 +348,10 @@
         pltpu.VMEM(block, BF16),
         pltpu.VMEM(block, BF16),
         pltpu.VMEM(block, F32),
+        pltpu.VMEM(block, BF16),
+        pltpu.VMEM(matrices, F32),
         dma((6 + 3 * ticks,)),
+        dma((len(WEIGHTS) + ticks - 1 + LATE_PIECES,)),
         dma((ticks, LATE_PIECES, 2)),
         dma((ticks, LATE_PIECES, 2)),
         dma((ticks - 1, len(WEIGHTS))),
@@ -353,14 +372,22 @@
             jax.ShapeDtypeStruct(incoming.shape, F32),
         ],
         in_specs=[hbm] * 7,
-        out_specs=[vmem, vmem],
+        out_specs=[anywhere, anywhere],
         scratch_shapes=scratch,
         compiler_params=pltpu.CompilerParams(
             collective_id=0, has_side_effects=True, vmem_limit_bytes=44 << 20
         ),
         name="layer_kernel",
     )(*(pltpu.with_memory_space_constraint(x, pltpu.HBM) for x in args))
-    return out, outgoing
+    return pl.pallas_call(
+        write_kernel,
+        out_shape=[jax.ShapeDtypeStruct(x.shape, x.dtype) for x in (out, outgoing)],
+        in_specs=[anywhere, anywhere],
+        out_specs=[anywhere, anywhere],
+        scratch_shapes=[dma((ticks + len(WEIGHTS),))],
+        compiler_params=pltpu.CompilerParams(vmem_limit_bytes=1 << 20),
+        name="write_kernel",
+    )(out, outgoing)
 
 
 def solution(mesh):

time: 73.6 us -> 74 us (level)
  Pallas kernels: 70.3 us -> 73.1 us
  local copies, waits for them, and re-layouts: 2.55 us -> 0 us
    unnamed x2 -> x0, local copies, waits for them, and re-layouts: 2.55 us -> none
    pallas_call x0 -> x1, Pallas kernels: none -> 1.96 us  [on_device(): pl.pallas_call(write_kernel, out_shape=[jax.ShapeDtypeStruct(x.shape, x.d...]
    pallas_call x1, Pallas kernels: 70.3 us -> 71.1 us  [on_device(): pl.pallas_call(layer_kernel, out_shape=[jax.ShapeDtypeStruct(queries.shap...]
where the time goes in v2:
time: 74 us; the launch traced here: 73.9 us
  Pallas kernels  73.1 us (99%)
  between operations  0.8 us (1%)
    pallas_call x1, Pallas kernels, on_device(): pl.pallas_call(layer_kernel, out_shape=[jax.ShapeDtypeStruct(queries.shap...  71.1 us
    pallas_call x1, Pallas kernels, on_device(): pl.pallas_call(write_kernel, out_shape=[jax.ShapeDtypeStruct(x.shape, x.d...  1.96 us

profile of v2, /device:TPU:0, one launch (start us, length us, event | category | flops | bytes accessed | tf_op | source)
XLA Modules:
  0.0 73.9 jit_solution(13998797703262785058)
XLA Ops:
  0.6 71.1 %layer_kernel.1 = (bf16[3,256,512]{2,1,0:T(8,128)(2,1)S(1)}, f32[1,1,3,512,512]{4,3,2,1,0:T(8,128)S(1)}) custom-call(bf16[3,256,512]{2,1,0:T(8,128)(2,1)} %q_hbm.1, bf16[4,256,512]{2,1,0:T(8,128)(2,1)} %k_hbm.1, bf16[4,256,512]{2,1,0:T(8,128)(2,1)} %v_hbm.1, f32[3,1,256]{2,1,0:T(1,128)} %bitcast.2, f32[1,512]{1,0:T(1,128)} %bitcast.3, ...), custom_call_target="tpu_custom_call" | custom-call | tf_op jit(solution)/shard_map/layer_kernel/pallas_call | solution.py:368
  71.7 2.0 %write_kernel.1 = (bf16[3,256,512]{2,1,0:T(8,128)(2,1)}, f32[1,1,3,512,512]{4,3,2,1,0:T(8,128)}) custom-call(bf16[3,256,512]{2,1,0:T(8,128)(2,1)S(1)} %get-tuple-element.4.out_ref, f32[1,1,3,512,512]{4,3,2,1,0:T(8,128)S(1)} %get-tuple-element.5.new_ref), custom_call_target="tpu_custom_call" | custom-call | tf_op jit(solution)/shard_map/write_kernel/pallas_call | solution.py:382

commit v3 on v2

--- a/solution.py
+++ b/solution.py
@@ -95,7 +95,7 @@
     q_hbm, k_hbm, v_hbm, rate_hbm, gain_hbm, ow_hbm, w_hbm,
     out_ref, new_ref,
     q, k, v, rate, gain, ow, w,
-    near, w_send, w_recv, z_send, z_recv, z_keep, z_fwd, z_last, z_own, out, new,
+    near, w_send, w_recv, z_send, z_recv, z_keep, z_fwd, z_last, out, new,
     in_sem, out_sem, near_s, near_r, w_s, w_r, z1_s, z1_r, z2_s, z2_r,
 ):
     ticks, rows, size = q.shape
@@ -151,6 +151,7 @@
 
     step = rows // LATE_PIECES
     cuts = [(i * step, (i + 1) * step) for i in reversed(range(LATE_PIECES))]
+    half = LATE_PIECES // 2
     leaving = []
 
     def leave(src, dst):
@@ -209,12 +210,12 @@
         z_first(t, a, b, j, 0).wait_recv()
         z_fwd[t, a:b] = (z_keep[t, 0, a:b].astype(F32) + z_recv[t, 0, a:b].astype(F32)).astype(BF16)
         z_second(t, a, b, j).start()
+
+    def finish(t, a, b, j):
         z_first(t, a, b, j, 1).wait_recv()
-        z_own[t, a:b] = z_keep[t, 1, a:b].astype(F32) + z_recv[t, 1, a:b].astype(F32)
-
-    def finish(t, a, b, j):
         z_second(t, a, b, j).wait_recv()
-        out[t, a:b] = (z_own[t, a:b] + z_last[t, a:b].astype(F32)).astype(BF16)
+        pair = z_keep[t, 1, a:b].astype(F32) + z_recv[t, 1, a:b].astype(F32)
+        out[t, a:b] = (pair + z_last[t, a:b].astype(F32)).astype(BF16)
         piece = pl.ds(a, b - a)
         leave(out.at[t, piece], out_ref.at[t, piece])
 
@@ -260,6 +261,8 @@
                 else:
                     new[i] = x
                     leave(new.at[i], new_ref.at[0, 0, i])
+                    if i == 1:
+                        pass_on(t, *cuts[half], half)
 
             fast_update(state, rounded, k[t], sv_of(t), store)
             if t < last:
@@ -271,6 +274,8 @@
                 get_gain.wait()
             return normed_apply(rounded, q[t], gain[...])
 
+        if t == 1:
+            pl.when(odd == 0)(lambda: pass_on(0, 0, rows, 0))
         if t < last:
             update()
         normed = apply()
@@ -278,14 +283,14 @@
             get_ow.wait()
         scores_own = own_scores(q[t], own[t])
         if t < last:
-            if t == 1:
-                pl.when(odd == 0)(lambda: pass_on(0, 0, rows, 0))
             for copy in near_copies(t):
                 copy.wait_recv()
             att = attend_rows(q[t], scores_own, prior[t], own[t], 0)
             project((att + normed).astype(BF16), t, 0, rows, 0)
             if t == 1:
                 pl.when(odd == 1)(lambda: pass_on(0, 0, rows, 0))
+            if t:
+                pass_on(t, 0, rows, 0)
             rounded = [arrived(t, i) for i in WEIGHTS]
             state = [lambda f=f: f().astype(F32) for f in rounded]
         else:
@@ -295,14 +300,13 @@
                     copy.wait_recv()
                 att = attend_rows(q[t, a:b], scores_own[a:b], prior[t], own[t], a)
                 project((att + normed[a:b]).astype(BF16), t, a, b, j)
-                if j == 0:
-                    for early in range(1, last):
-                        pass_on(early, 0, rows, 0)
+            for j in range(half):
+                pass_on(t, *cuts[j], j)
             update()
+            for j in range(half + 1, LATE_PIECES):
+                pass_on(t, *cuts[j], j)
             for early in range(last):
                 finish(early, 0, rows, 0)
-            for j, (a, b) in enumerate(cuts):
-                pass_on(t, a, b, j)
             for j, (a, b) in enumerate(cuts):
                 finish(t, a, b, j)
     for copy in leaving:
@@ -347,7 +351,6 @@
         pltpu.VMEM((ticks, 2, rows, size), BF16),
         pltpu.VMEM(block, BF16),
         pltpu.VMEM(block, BF16),
-        pltpu.VMEM(block, F32),
         pltpu.VMEM(block, BF16),
         pltpu.VMEM(matrices, F32),
         dma((6 + 3 * ticks,)),

time: 74 us -> 70.9 us (0.958)
  Pallas kernels: 73.1 us -> 70 us
    pallas_call x1, Pallas kernels: 71.1 us -> 68 us  [on_device(): pl.pallas_call(layer_kernel, out_shape=[jax.ShapeDtypeStruct(queries.shap...]
where the time goes in v3:
time: 70.9 us; the launch traced here: 70.8 us
  Pallas kernels  70 us (99%)
  between operations  0.8 us (1%)
    pallas_call x1, Pallas kernels, on_device(): pl.pallas_call(layer_kernel, out_shape=[jax.ShapeDtypeStruct(queries.shap...  68 us
    pallas_call x1, Pallas kernels, on_device(): pl.pallas_call(write_kernel, out_shape=[jax.ShapeDtypeStruct(x.shape, x.d...  1.96 us

profile of v3, /device:TPU:0, one launch (start us, length us, event | category | flops | bytes accessed | tf_op | source)
XLA Modules:
  0.0 70.8 jit_solution(401046879240602631)
XLA Ops:
  0.6 68.0 %layer_kernel.1 = (bf16[3,256,512]{2,1,0:T(8,128)(2,1)S(1)}, f32[1,1,3,512,512]{4,3,2,1,0:T(8,128)S(1)}) custom-call(bf16[3,256,512]{2,1,0:T(8,128)(2,1)} %q_hbm.1, bf16[4,256,512]{2,1,0:T(8,128)(2,1)} %k_hbm.1, bf16[4,256,512]{2,1,0:T(8,128)(2,1)} %v_hbm.1, f32[3,1,256]{2,1,0:T(1,128)} %bitcast.2, f32[1,512]{1,0:T(1,128)} %bitcast.3, ...), custom_call_target="tpu_custom_call" | custom-call | tf_op jit(solution)/shard_map/layer_kernel/pallas_call | solution.py:371
  68.7 2.0 %write_kernel.1 = (bf16[3,256,512]{2,1,0:T(8,128)(2,1)}, f32[1,1,3,512,512]{4,3,2,1,0:T(8,128)}) custom-call(bf16[3,256,512]{2,1,0:T(8,128)(2,1)S(1)} %get-tuple-element.4.out_ref, f32[1,1,3,512,512]{4,3,2,1,0:T(8,128)S(1)} %get-tuple-element.5.new_ref), custom_call_target="tpu_custom_call" | custom-call | tf_op jit(solution)/shard_map/write_kernel/pallas_call | solution.py:385

commit v4 on v3

--- a/solution.py
+++ b/solution.py
@@ -96,7 +96,7 @@
     out_ref, new_ref,
     q, k, v, rate, gain, ow, w,
     near, w_send, w_recv, z_send, z_recv, z_keep, z_fwd, z_last, out, new,
-    in_sem, out_sem, near_s, near_r, w_s, w_r, z1_s, z1_r, z2_s, z2_r,
+    in_sem, near_s, near_r, w_s, w_r, z1_s, z1_r, z2_s, z2_r,
 ):
     ticks, rows, size = q.shape
     last = ticks - 1
@@ -138,16 +138,13 @@
         get_q[t] = load(q_hbm.at[t], q.at[t])
     pl.semaphore_wait(barrier, 4)
 
-    sent = []
-
     def remote(src, dst, ss, rs, who):
         return pltpu.make_async_remote_copy(
             src_ref=src, dst_ref=dst, send_sem=ss, recv_sem=rs, device_id=who, device_id_type=MESH
         )
 
-    def push(copy):
-        copy.start()
-        sent.append(copy)
+    def wait_all_sent(buffer, sem):
+        remote(buffer, buffer, sem, w_r.at[0, 0], {"seq": nxt}).wait_send()
 
     step = rows // LATE_PIECES
     cuts = [(i * step, (i + 1) * step) for i in reversed(range(LATE_PIECES))]
@@ -155,29 +152,27 @@
     leaving = []
 
     def leave(src, dst):
-        copy = pltpu.make_async_copy(src, dst, out_sem.at[len(leaving)])
+        copy = pltpu.make_async_copy(src, dst, in_sem.at[len(leaving)])
         copy.start()
         leaving.append(copy)
 
-    def near_copies(t):
-        found = []
-        for j, (a, b) in enumerate(cuts if t == last else [(0, rows)]):
+    def pieces(t):
+        return cuts if t == last else [(0, rows)]
+
+    def send_near(t):
+        for j, (a, b) in enumerate(pieces(t)):
             for i, hbm in enumerate((k_hbm, v_hbm)):
-                at = (t, j, i)
-                found.append(
-                    remote(
-                        hbm.at[t, pl.ds(a, b - a)], near.at[t, i, pl.ds(a, b - a)],
-                        near_s.at[at], near_r.at[at], {"seq": nxt},
-                    )
-                )
-        return found
-
-    def send_near(t):
-        for copy in near_copies(t):
-            push(copy)
+                piece = pl.ds(a, b - a)
+                remote(
+                    hbm.at[t, piece], near.at[t, i, piece], near_s, near_r.at[t + j], {"seq": nxt}
+                ).start()
+
+    def wait_near(t, a, b, j):
+        both = near.at[t, :, pl.ds(a, b - a)]
+        remote(both, both, near_s, near_r.at[t + j], {"seq": nxt}).wait_recv()
 
     def w_copy(t, i):
-        return remote(w_send.at[t, i], w_recv.at[t, i], w_s.at[t, i], w_r.at[t, i], {"seq": nxt})
+        return remote(w_send.at[t, i], w_recv.at[t, i], w_s, w_r.at[t, i], {"seq": nxt})
 
     def sv_of(t):
         column = jnp.broadcast_to(rate[t], (8, rows)).T[:, :1]
@@ -186,13 +181,13 @@
     def z_first(t, a, b, j, i):
         return remote(
             z_send.at[t, i, pl.ds(a, b - a)], z_recv.at[t, i, pl.ds(a, b - a)],
-            z1_s.at[t, j, i], z1_r.at[t, j, i], {"head": first},
+            z1_s, z1_r.at[t + j, i], {"head": first},
         )
 
     def z_second(t, a, b, j):
         return remote(
             z_fwd.at[t, pl.ds(a, b - a)], z_last.at[t, pl.ds(a, b - a)],
-            z2_s.at[t, j], z2_r.at[t, j], {"head": second},
+            z2_s, z2_r.at[t + j], {"head": second},
         )
 
     def project(combined, t, a, b, j):
@@ -202,7 +197,7 @@
 
         for i, target in enumerate((across, first)):
             z_send[t, i, a:b] = piece(target)
-            push(z_first(t, a, b, j, i))
+            z_first(t, a, b, j, i).start()
         z_keep[t, 0, a:b] = piece(second)
         z_keep[t, 1, a:b] = piece(h)
 
@@ -257,7 +252,7 @@
             def store(i, x):
                 if t < last:
                     w_send[t, i] = x.astype(BF16)
-                    push(w_copy(t, i))
+                    w_copy(t, i).start()
                 else:
                     new[i] = x
                     leave(new.at[i], new_ref.at[0, 0, i])
@@ -283,8 +278,7 @@
             get_ow.wait()
         scores_own = own_scores(q[t], own[t])
         if t < last:
-            for copy in near_copies(t):
-                copy.wait_recv()
+            wait_near(t, 0, rows, 0)
             att = attend_rows(q[t], scores_own, prior[t], own[t], 0)
             project((att + normed).astype(BF16), t, 0, rows, 0)
             if t == 1:
@@ -294,10 +288,8 @@
             rounded = [arrived(t, i) for i in WEIGHTS]
             state = [lambda f=f: f().astype(F32) for f in rounded]
         else:
-            copies = near_copies(t)
             for j, (a, b) in enumerate(cuts):
-                for copy in copies[2 * j : 2 * j + 2]:
-                    copy.wait_recv()
+                wait_near(t, a, b, j)
                 att = attend_rows(q[t, a:b], scores_own[a:b], prior[t], own[t], a)
                 project((att + normed[a:b]).astype(BF16), t, a, b, j)
             for j in range(half):
@@ -311,11 +303,8 @@
                 finish(t, a, b, j)
     for copy in leaving:
         copy.wait()
-    for copy in sent:
-        copy.wait_send()
-    for t in range(ticks):
-        for j, (a, b) in enumerate(cuts if t == last else [(0, rows)]):
-            z_second(t, a, b, j).wait_send()
+    for buffer, sem in ((near, near_s), (w_send, w_s), (z_send, z1_s), (z_fwd, z2_s)):
+        wait_all_sent(buffer, sem)
 
 
 def write_kernel(out_ref, new_ref, out_to, new_to, sem):
@@ -354,15 +343,14 @@
         pltpu.VMEM(block, BF16),
         pltpu.VMEM(matrices, F32),
         dma((6 + 3 * ticks,)),
-        dma((len(WEIGHTS) + ticks - 1 + LATE_PIECES,)),
-        dma((ticks, LATE_PIECES, 2)),
-        dma((ticks, LATE_PIECES, 2)),
+        dma,
+        dma((ticks - 1 + LATE_PIECES,)),
+        dma,
         dma((ticks - 1, len(WEIGHTS))),
-        dma((ticks - 1, len(WEIGHTS))),
-        dma((ticks, LATE_PIECES, 2)),
-        dma((ticks, LATE_PIECES, 2)),
-        dma((ticks, LATE_PIECES)),
-        dma((ticks, LATE_PIECES)),
+        dma,
+        dma((ticks - 1 + LATE_PIECES, 2)),
+        dma,
+        dma((ticks - 1 + LATE_PIECES,)),
     ]
     args = (
         queries, key_vectors, values, learn_rates.transpose(0, 2, 1), norm_gain.reshape(1, size),

time: 70.9 us -> 69.9 us (0.986)
  Pallas kernels: 70 us -> 69 us
    pallas_call x1, Pallas kernels: 68 us -> 67 us  [on_device(): pl.pallas_call(layer_kernel, out_shape=[jax.ShapeDtypeStruct(queries.shap...]
where the time goes in v4:
time: 69.9 us; the launch traced here: 69.8 us
  Pallas kernels  69 us (99%)
  between operations  0.8 us (1%)
    pallas_call x1, Pallas kernels, on_device(): pl.pallas_call(layer_kernel, out_shape=[jax.ShapeDtypeStruct(queries.shap...  67 us
    pallas_call x1, Pallas kernels, on_device(): pl.pallas_call(write_kernel, out_shape=[jax.ShapeDtypeStruct(x.shape, x.d...  1.96 us

profile of v4, /device:TPU:0, one launch (start us, length us, event | category | flops | bytes accessed | tf_op | source)
XLA Modules:
  0.0 69.8 jit_solution(14848062681571901644)
XLA Ops:
  0.6 67.0 %layer_kernel.1 = (bf16[3,256,512]{2,1,0:T(8,128)(2,1)S(1)}, f32[1,1,3,512,512]{4,3,2,1,0:T(8,128)S(1)}) custom-call(bf16[3,256,512]{2,1,0:T(8,128)(2,1)} %q_hbm.1, bf16[4,256,512]{2,1,0:T(8,128)(2,1)} %k_hbm.1, bf16[4,256,512]{2,1,0:T(8,128)(2,1)} %v_hbm.1, f32[3,1,256]{2,1,0:T(1,128)} %bitcast.2, f32[1,512]{1,0:T(1,128)} %bitcast.3, ...), custom_call_target="tpu_custom_call" | custom-call | tf_op jit(solution)/shard_map/layer_kernel/pallas_call | solution.py:359
  67.6 2.0 %write_kernel.1 = (bf16[3,256,512]{2,1,0:T(8,128)(2,1)}, f32[1,1,3,512,512]{4,3,2,1,0:T(8,128)}) custom-call(bf16[3,256,512]{2,1,0:T(8,128)(2,1)S(1)} %get-tuple-element.4.out_ref, f32[1,1,3,512,512]{4,3,2,1,0:T(8,128)S(1)} %get-tuple-element.5.new_ref), custom_call_target="tpu_custom_call" | custom-call | tf_op jit(solution)/shard_map/write_kernel/pallas_call | solution.py:373
